TPU v7x, 512 devices: a whole 4x8x8 slice. The times are simulated.
512 devices in a mesh: sub: 64 (over z, y), tm: 8 (over x, core).
Axes of the slice: x: 4, y: 8, z: 8, core: 2. Of those that a mesh axis runs over, the one named last changes fastest.
Arguments:
- data: bfloat16 [1, 16384, 2048], P(None, 'sub', 'tm'), may hold values from -6 to 6
- delays: int32 [16384], P('sub'), may hold values from 0 to 15, as said below
- offsets: int32 [2048, 1024], P('sub'), may hold values from 0 to 96, as said below
- widths: int32 [8], replicated, may hold values from 1 to 128, as said below
Outputs:
- boxcars: float32 [2048, 1, 8, 2048], P('sub', None, None, 'tm')
Inputs may be any that keep to these rules, and one draw needn't show every extreme that they name: `delays`: some channel has delay 16 - 1. `offsets`: some entry equals 96 and some entry equals 0. `widths`: some entry equals 128.
All inputs are finite; a program needn't handle non-finite values.
Results may differ from a plain program's by a relative error of at most 0.0048.
Values may be sent and summed in bfloat16 or wider, within the bound.
A program may use at most 64 MiB of HBM per device.

v0:
```python
import math

import jax
import jax.numpy as jnp
from jax import lax
from jax.sharding import PartitionSpec as P

WMAX = 128
DCH = 16
OMAX = 96


def passed_along(value, axis, steps):
    count = lax.axis_size(axis)
    initial, last = (max(0, -steps), min(count, count - steps))
    return lax.ppermute(value, axis, [(source, source + steps) for source in range(initial, last)])


def series_of(padded_series_block, delays, sub_count, count):
    chans = padded_series_block.shape[1]
    per_sub = chans // sub_count
    owner = jnp.arange(chans, dtype=jnp.int32) // per_sub
    member = owner[None, :] == jnp.arange(sub_count, dtype=jnp.int32)[:, None]
    running = jnp.zeros((padded_series_block.shape[0], sub_count, count), jnp.float32)
    for delay in range(DCH):
        select = (member & (delays[None, :] == delay)).astype(jnp.bfloat16)
        running = running + jnp.einsum(
            "sc,bct->bst",
            select,
            padded_series_block[:, :, delay : delay + count],
            preferred_element_type=jnp.float32,
        )
    return running.astype(jnp.bfloat16)


def hankel_of(series, length):
    return jnp.stack([series[:, :, lag : lag + length] for lag in range(OMAX + 1)], axis=2)


def project(lag_rows, hankel, scale):
    onehot = (lag_rows[:, :, None] == jnp.arange(OMAX + 1, dtype=jnp.int32)[None, None, :]).astype(
        jnp.bfloat16
    )
    return jnp.einsum("msk,bskt->mbt", onehot, hankel, preferred_element_type=jnp.float32) * scale


def per_device(data, delays, offsets, widths):
    beams, chans, length = data.shape
    dm_dev = offsets.shape[0]
    nsub = offsets.shape[1]
    groups = lax.axis_size("sub")
    sub_dev = nsub // groups
    scale = 1.0 / math.sqrt(chans * groups)
    extra = 0
    out_len = length + extra
    trailing_rows = passed_along(data[:, :, : OMAX + DCH - 1 + extra], "tm", -1)
    series = series_of(
        jnp.concatenate([data, trailing_rows], axis=2), delays, sub_dev, out_len + OMAX
    )
    table = lax.all_to_all(offsets, "sub", split_axis=1, concat_axis=0, tiled=True)
    hankel = hankel_of(series, out_len)
    block = math.gcd(lax.axis_size("sub") * dm_dev, 256)

    def one_block(block_index):
        lag_rows = lax.dynamic_slice_in_dim(table, block_index * block, block, 0)
        return project(lag_rows, hankel, scale)

    blocks = lax.map(one_block, jnp.arange(lax.axis_size("sub") * dm_dev // block, dtype=jnp.int32))
    channel_totals = lax.psum_scatter(
        blocks.reshape(lax.axis_size("sub") * dm_dev, beams, out_len),
        "sub",
        scatter_dimension=0,
        tiled=True,
    )
    dedispersed = channel_totals.astype(jnp.bfloat16)
    later_rows = passed_along(dedispersed[:, :, : WMAX - 1], "tm", -1)
    padded_series_block = jnp.concatenate([dedispersed, later_rows], axis=2)
    lag = (
        jnp.arange(padded_series_block.shape[2], dtype=jnp.int32)[:, None]
        - jnp.arange(length, dtype=jnp.int32)[None, :]
    )
    subband_weight_matrix = ((lag[None] >= 0) & (lag[None] < widths[:, None, None])).astype(
        jnp.bfloat16
    )
    filtered = jnp.einsum(
        "syh,qho->syqo",
        padded_series_block,
        subband_weight_matrix,
        preferred_element_type=jnp.float32,
    )
    return filtered / jnp.sqrt(widths.astype(jnp.float32))[None, None, :, None]


def solution(mesh):
    placed = (P(None, "sub", "tm"), P("sub"), P("sub", None), P())
    return jax.shard_map(
        per_device,
        mesh=mesh,
        in_specs=placed,
        out_specs=P("sub", None, None, "tm"),
        check_vma=False,
    )
```

profile of v0, /device:TPU:1, one launch (start us, length us, event | category | flops | bytes accessed | tf_op | source)
XLA Modules:
  0.0 329.2 jit_solution(11351075567384402200)
XLA Ops:
  6.5 0.8 slice.345
  7.4 8.7 %collective-permute-start = (bf16[1,256,111]{2,1,0:T(8,128)(2,1)S(1)}, bf16[1,256,111]{2,1,0:T(8,128)(2,1)S(1)}, u32[]{:S(2)}, u32[]{:S(2)}) collective-permute-start(bf16[1,256,111]{2,1,0:T(8,128)(2,1)S(1)} %slice.345), channel_id=1, source_target_pairs={{1,0},{2,1},{3,2},{4,3},{5,4},{6,5},{7,6},{9,8},{10,9},{11,10},{12... | collective-permute-start | bytes 170504 | tf_op jit(solution)/shard_map/ppermute | solution.py:16
  16.1 1.1 copy.8
  17.2 0.9 reshape.191
  18.1 11.0 %all-to-all-start = ((s32[64,1,512]{2,1,0:T(1,128)}), s32[64,1,512]{2,1,0:T(1,128)S(1)}, u32[]{:S(2)}, u32[]{:S(2)}) async-start(s32[64,1,512]{2,1,0:T(1,128)} %reshape.191), calls=%async_computation | async-start | bytes 262144 | tf_op jit(solution)/shard_map/all_to_all | solution.py:60
  29.2 0.9 constant_dynamic-update-slice_fusion.1
  30.1 0.7 broadcast_compare_fusion.14
  42.9 0.9 reduce
  44.5 20.8 %while.10 = (s32[]{:T(128)}, f32[8,256,1,256]{3,1,2,0:T(8,128)}, s32[8]{0:T(128)S(1)}, s32[2048,16]{0,1:T(8,128)S(1)}, bf16[1,16,97,256]{3,2,1,0:T(8,128)(2,1)S(...) while((s32[]{:T(128)}, f32[8,256,1,256]{3,1,2,0:T(8,128)}, s32[8]{0:T(128)S(1)}, ...), condition=%wide.region_1.2_spmd, body=%wide.region_0.1_spmd.sunk | while | flops 203886592 | bytes 1106587 | solution.py:68
  44.5 0.6 dynamic_slice.11
  45.8 1.3 fusion.115
  47.1 0.6 dynamic_slice.11
  48.4 1.3 fusion.115
  49.7 0.6 dynamic_slice.11
  51.0 1.3 fusion.115
  52.3 0.6 dynamic_slice.11
  53.5 1.3 fusion.115
  54.9 0.6 dynamic_slice.11
  56.1 1.3 fusion.115
  57.5 0.6 dynamic_slice.11
  58.7 1.4 fusion.115
  60.1 0.6 dynamic_slice.11
  61.3 1.3 fusion.115
  62.7 0.6 dynamic_slice.11
  63.9 1.3 fusion.115
  65.3 0.6 copy-done
  65.9 244.2 %reduce-scatter.2.cloned.1.call-done = f32[32,1,256]{2,0,1:T(8,128)} async-done(((f32[2048,1,256]{2,0,1:T(8,128)}), f32[32,1,256]{2,0,1:T(8,128)}) %reduce-scatter.2.cloned.1.call-update) | async-done | bytes 32784 | tf_op jit(solution)/shard_map/reduce_scatter | solution.py:69
  310.1 0.8 convert_element_type.7
  310.9 7.4 %collective-permute-start.1 = (bf16[32,1,127]{2,0,1:T(8,128)(2,1)S(1)}, bf16[32,1,127]{2,0,1:T(8,128)(2,1)S(1)}, u32[]{:S(2)}, u32[]{:S(2)}) collective-permute-start(bf16[32,1,127]{2,0,1:T(8,128)(2,1)S(1)} %slice.573), channel_id=1, source_target_pairs={{1,0},{2,1},{3,2},{4,3},{5,4},{6,5},{7,6},{9,8},{10,9},{11,10},{12... | collective-permute-start | bytes 24392 | tf_op jit(solution)/shard_map/ppermute | solution.py:16
  318.4 2.4 collective-permute-done.1
  320.7 0.8 fusion.12
  321.5 0.9 copy.11
  (140 shorter events, 12.8 us)
Async XLA Ops:
  7.4 23.4 %collective-permute-start = (bf16[1,256,111]{2,1,0:T(8,128)(2,1)S(1)}, bf16[1,256,111]{2,1,0:T(8,128)(2,1)S(1)}, u32[]{:S(2)}, u32[]{:S(2)}) collective-permute-start(bf16[1,256,111]{2,1,0:T(8,128)(2,1)S(1)} %slice.345), channel_id=1, source_target_pairs={{1,0},{2,1},{3,2},{4,3},{5,4},{6,5},{7,6},{9,8},{10,9},{11,10},{12... | collective-permute-start | bytes 170504 | tf_op jit(solution)/shard_map/ppermute | solution.py:16
  18.1 24.2 %all-to-all-start = ((s32[64,1,512]{2,1,0:T(1,128)}), s32[64,1,512]{2,1,0:T(1,128)S(1)}, u32[]{:S(2)}, u32[]{:S(2)}) async-start(s32[64,1,512]{2,1,0:T(1,128)} %reshape.191), calls=%async_computation | async-start | bytes 262144 | tf_op jit(solution)/shard_map/all_to_all | solution.py:60
  29.1 281.0 %reduce-scatter.2.cloned.1.call-start = ((), (), s32[]{:S(2)}) async-start(), calls=%async_computation.2 | async-start | bytes 2129920 | tf_op jit(solution)/shard_map/reduce_scatter | solution.py:69
  65.3 0.7 copy-start
  310.9 9.8 %collective-permute-start.1 = (bf16[32,1,127]{2,0,1:T(8,128)(2,1)S(1)}, bf16[32,1,127]{2,0,1:T(8,128)(2,1)S(1)}, u32[]{:S(2)}, u32[]{:S(2)}) collective-permute-start(bf16[32,1,127]{2,0,1:T(8,128)(2,1)S(1)} %slice.573), channel_id=1, source_target_pairs={{1,0},{2,1},{3,2},{4,3},{5,4},{6,5},{7,6},{9,8},{10,9},{11,10},{12... | collective-permute-start | bytes 24392 | tf_op jit(solution)/shard_map/ppermute | solution.py:16
Sparse Core Ops, SparseCore 0:
  65.4 244.6 reduce-scatter.1
where the time goes:
time: 330 us; the launch traced here: 329 us
  waiting for transfers between devices  247 us (75%)
  starting transfers between devices  27.1 us (8%)
  local copies, waits for them, and re-layouts  18.8 us (6%)
  matrix products  15.3 us (5%)
  between operations  13.7 us (4%)
  loops' own time  5.33 us (2%)
    reduce_scatter x1, waiting for transfers between devices, per_device(): lax.psum_scatter(blocks.reshape(lax.axis_size('sub') * dm_dev, beams, out...  244 us
    ppermute x2, starting transfers between devices, passed_along(): lax.ppermute(value, axis, [(source, source + steps) for source in range(i...  16.1 us
    all_to_all x1, starting transfers between devices, per_device(): lax.all_to_all(offsets, 'sub', split_axis=1, concat_axis=0, tiled=True)  11 us
    unnamed x102, local copies, waits for them, and re-layouts  10.9 us
    dot_general x8, matrix products, project(): jnp.einsum('msk,bskt->mbt', onehot, hankel, preferred_element_type=jnp.fl...  10.7 us
  transfers between devices with their start and end apart: 4, of which 2 were waited for; matrix products, arithmetic and copies ran while one was open for 5% of the time, Pallas kernels for 0%

commit v1 on v0

v1 whole, which is shorter than its diff:
```python
import functools
import math

import jax
import jax.numpy as jnp
from jax import lax
from jax.experimental import pallas as pl
from jax.experimental.pallas import tpu as pltpu
from jax.sharding import PartitionSpec as P

WMAX = 128
DCH = 16
OMAX = 96
RING = 8
LANES = 128
EDGE = 112
STEP = 8
MESH = pl.DeviceIdType.MESH
FAR_FIRST = (4, 3, 5, 2, 6, 1, 7)
NEAR_FIRST = (1, 7, 2, 6, 3, 5, 4)


def iota(shape, dim):
    return lax.broadcasted_iota(jnp.int32, shape, dim)


def dedisperse_kernel(
    scale,
    blocks,
    data_ref,
    delays_ref,
    offsets_ref,
    out_ref,
    lag_out,
    lags,
    own_buf,
    halo_out,
    halo_buf,
    series_buf,
    part_buf,
    sum_buf,
    send_own,
    recv_own,
    send_halo,
    recv_halo,
    send_lag,
    recv_lag,
    send_part,
    recv_part,
    send_edge,
    recv_edge,
):
    sub = lax.axis_index("sub")
    tm = lax.axis_index("tm")
    z, y = sub // RING, sub % RING
    chans, length = data_ref.shape
    per = own_buf.shape[1]
    dms = lag_out.shape[1]
    first, last = tm == 0, tm == blocks - 1

    def along_y(d):
        return z * RING + lax.rem(y + d, RING)

    def along_z(d):
        return lax.rem(z + d, RING) * RING + y

    barrier = pltpu.get_barrier_semaphore()

    def greet(block, with_self):
        for d in range(0 if with_self else 1, RING):
            pl.semaphore_signal(barrier, inc=1, device_id=(along_y(d), block), device_id_type=MESH)
        for d in range(1, RING):
            pl.semaphore_signal(barrier, inc=1, device_id=(along_z(d), block), device_id_type=MESH)

    greet(tm, False)

    @pl.when(tm > 0)
    def _():
        greet(tm - 1, True)

    @pl.when(tm < blocks - 1)
    def _():
        greet(tm + 1, True)

    for g in range(RING):
        lag_out[g] = offsets_ref[:, g * LANES : (g + 1) * LANES].astype(jnp.float32).astype(jnp.bfloat16)
    lags[z] = lag_out[z]

    eye = iota((chans, chans), 0) == iota((chans, chans), 1)
    diagonal = jnp.where(eye, delays_ref[...], 0).astype(jnp.float32).astype(jnp.bfloat16)
    delay = jnp.dot(diagonal, jnp.ones((chans, LANES), jnp.bfloat16), preferred_element_type=jnp.float32)
    delay = delay.astype(jnp.int32)
    delay = jnp.concatenate([delay] * 3, axis=1)
    wide = length + LANES
    moved = jnp.concatenate(
        [jnp.zeros((chans, LANES), jnp.float32), data_ref[...].astype(jnp.float32)], axis=1
    )
    for bit in (1, 2, 4, 8):
        moved = jnp.where((delay & bit) != 0, pltpu.roll(moved, wide - bit, 1), moved)
    member = (iota((per, chans), 1) // (chans // per) == iota((per, chans), 0)).astype(jnp.float32)
    summed = jnp.dot(
        member.astype(jnp.bfloat16), moved.astype(jnp.bfloat16), preferred_element_type=jnp.float32
    )
    own_buf[y] = summed[:, LANES:].astype(jnp.bfloat16)
    halo_out[...] = jnp.where(
        iota((per, LANES), 1) < EDGE, summed[:, LANES : 2 * LANES], summed[:, :LANES]
    ).astype(jnp.bfloat16)

    pl.semaphore_wait(
        barrier,
        2 * (RING - 1)
        + (2 * RING - 1) * (jnp.where(first, 0, 1) + jnp.where(last, 0, 1)),
    )

    def lag_copy(d, source):
        g = lax.rem(z + d, RING)
        return pltpu.make_async_remote_copy(
            src_ref=lag_out.at[g],
            dst_ref=lags.at[source],
            send_sem=send_lag.at[d],
            recv_sem=recv_lag.at[source],
            device_id=(along_z(d), tm),
            device_id_type=MESH,
        )

    def own_copy(d, source):
        return pltpu.make_async_remote_copy(
            src_ref=own_buf.at[y],
            dst_ref=own_buf.at[source],
            send_sem=send_own.at[d],
            recv_sem=recv_own.at[source],
            device_id=(along_y(d), tm),
            device_id_type=MESH,
        )

    def halo_copy(d, source):
        return pltpu.make_async_remote_copy(
            src_ref=halo_out,
            dst_ref=halo_buf.at[source],
            send_sem=send_halo.at[d],
            recv_sem=recv_halo.at[source],
            device_id=(along_y(d), tm - 1),
            device_id_type=MESH,
        )

    for d in FAR_FIRST:
        own_copy(d, y).start()
        lag_copy(d, z).start()

    @pl.when(tm > 0)
    def _():
        for d in FAR_FIRST + (0,):
            halo_copy(d, y).start()

    @pl.when(last)
    def _():
        halo_buf[...] = jnp.zeros(halo_buf.shape, halo_buf.dtype)

    for d in NEAR_FIRST:
        lag_copy(d, lax.rem(z + d, RING)).wait_recv()
        own_copy(d, lax.rem(y + d, RING)).wait_recv()

    @pl.when(jnp.logical_not(last))
    def _():
        for d in (0,) + NEAR_FIRST:
            halo_copy(d, lax.rem(y + d, RING)).wait_recv()

    rows = RING * per
    own = own_buf[...].reshape(rows, length)
    halo = halo_buf[...].reshape(rows, LANES)
    edge = jnp.where(iota((rows, LANES), 1) >= EDGE, halo.astype(jnp.float32), 0.0)
    tail = (own[:, length - LANES :].astype(jnp.float32) + edge).astype(jnp.bfloat16)
    series_buf[...] = jnp.concatenate([own[:, : length - LANES], tail, halo], axis=1)

    table = lags[...].reshape(RING * dms, rows)

    def some_lags(block, total):
        base = block * STEP
        here = pltpu.roll(series_buf[...], wide - base, 1)
        masks, windows = [], []
        for j in range(STEP):
            lag = (base + j).astype(jnp.float32).astype(jnp.bfloat16)
            masks.append(jnp.where(table == lag, jnp.bfloat16(1), jnp.bfloat16(0)))
            windows.append(here[:, j : j + length])
        return total + jnp.dot(
            jnp.concatenate(masks, axis=1),
            jnp.concatenate(windows, axis=0),
            preferred_element_type=jnp.float32,
        )

    total = lax.fori_loop(
        0, pl.cdiv(OMAX + 1, STEP), some_lags, jnp.zeros((RING * dms, length), jnp.float32)
    )
    part_buf[...] = total.astype(jnp.bfloat16).reshape(RING, dms, length)

    def part_copy(d, source):
        g = lax.rem(z + d, RING)
        return pltpu.make_async_remote_copy(
            src_ref=part_buf.at[g],
            dst_ref=sum_buf.at[source, :, pl.ds(0, length)],
            send_sem=send_part.at[d],
            recv_sem=recv_part.at[source],
            device_id=(along_z(d), tm),
            device_id_type=MESH,
        )

    def edge_copy(d, source):
        g = lax.rem(z + d, RING)
        return pltpu.make_async_remote_copy(
            src_ref=part_buf.at[g, :, pl.ds(0, LANES)],
            dst_ref=sum_buf.at[source, :, pl.ds(length, LANES)],
            send_sem=send_edge.at[d],
            recv_sem=recv_edge.at[source],
            device_id=(along_z(d), tm - 1),
            device_id_type=MESH,
        )

    for d in FAR_FIRST:
        part_copy(d, z).start()

    @pl.when(tm > 0)
    def _():
        for d in FAR_FIRST + (0,):
            edge_copy(d, z).start()

    @pl.when(last)
    def _():
        sum_buf[:, :, length:] = jnp.zeros((RING, dms, LANES), jnp.bfloat16)

    sum_buf[z, :, :length] = part_buf[z]

    for d in NEAR_FIRST:
        part_copy(d, lax.rem(z + d, RING)).wait_recv()

    @pl.when(jnp.logical_not(last))
    def _():
        for d in (0,) + NEAR_FIRST:
            edge_copy(d, lax.rem(z + d, RING)).wait_recv()

    added = sum_buf[0].astype(jnp.float32)
    for g in range(1, RING):
        added = added + sum_buf[g].astype(jnp.float32)
    out_ref[...] = (added * scale).astype(jnp.bfloat16)

    for d in NEAR_FIRST:
        own_copy(d, y).wait_send()
        lag_copy(d, z).wait_send()
        part_copy(d, z).wait_send()

    @pl.when(tm > 0)
    def _():
        for d in (0,) + NEAR_FIRST:
            halo_copy(d, y).wait_send()
            edge_copy(d, z).wait_send()


def boxcar_kernel(widths_ref, series_ref, out_ref, woven):
    span = series_ref.shape[1]
    length = out_ref.shape[1]
    count = widths_ref.shape[0]
    dms = series_ref.shape[0]
    lag = iota((span, length), 0) - iota((span, length), 1)
    for i in range(count):
        width = widths_ref[i]
        window = jnp.where((lag >= 0) & (lag < width), 1.0, 0.0).astype(jnp.bfloat16)
        total = jnp.dot(series_ref[...], window, preferred_element_type=jnp.float32)
        root = jnp.sqrt(jnp.full((dms, length), width, jnp.int32).astype(jnp.float32))
        total = total / root
        for h in range(length // LANES):
            woven[h, pl.ds(i, dms, stride=count), :] = total[:, h * LANES : (h + 1) * LANES]
    for h in range(length // LANES):
        out_ref[:, h * LANES : (h + 1) * LANES] = woven[h]


def solution(mesh):
    blocks = mesh.shape["tm"]

    def per_device(data, delays, offsets, widths):
        _, chans, length = data.shape
        dms, nsub = offsets.shape
        groups = lax.axis_size("sub")
        per = nsub // groups
        scale = 1.0 / math.sqrt(chans * groups)
        vmem = pl.BlockSpec(memory_space=pltpu.VMEM)
        bf16 = jnp.bfloat16
        dma = pltpu.SemaphoreType.DMA((RING,))
        series = pl.pallas_call(
            functools.partial(dedisperse_kernel, scale, blocks),
            out_shape=jax.ShapeDtypeStruct((dms, length + LANES), bf16),
            in_specs=[vmem] * 3,
            out_specs=vmem,
            scratch_shapes=[
                pltpu.VMEM((RING, dms, LANES), bf16),
                pltpu.VMEM((RING, dms, LANES), bf16),
                pltpu.VMEM((RING, per, length), bf16),
                pltpu.VMEM((per, LANES), bf16),
                pltpu.VMEM((RING, per, LANES), bf16),
                pltpu.VMEM((RING * per, length + LANES), bf16),
                pltpu.VMEM((RING, dms, length), bf16),
                pltpu.VMEM((RING, dms, length + LANES), bf16),
            ]
            + [dma] * 10,
            compiler_params=pltpu.CompilerParams(collective_id=0, has_side_effects=True),
        )(data[0], delays[None, :], offsets)
        count = widths.shape[0]
        out = pl.pallas_call(
            boxcar_kernel,
            out_shape=jax.ShapeDtypeStruct((dms * count, length), jnp.float32),
            in_specs=[pl.BlockSpec(memory_space=pltpu.SMEM), vmem],
            out_specs=vmem,
            scratch_shapes=[pltpu.VMEM((length // LANES, dms * count, LANES), jnp.float32)],
        )(widths, series)
        return out.reshape(dms, 1, count, length)

    placed = (P(None, "sub", "tm"), P("sub"), P("sub", None), P())
    return jax.shard_map(
        per_device,
        mesh=mesh,
        in_specs=placed,
        out_specs=P("sub", None, None, "tm"),
        check_vma=False,
    )
```

time: 330 us -> 40.6 us (0.12)
  waiting for transfers between devices: 247 us -> 0 us
  Pallas kernels: 0 us -> 40.4 us
  starting transfers between devices: 27.1 us -> 0 us
  local copies, waits for them, and re-layouts: 18.8 us -> 0 us
  matrix products: 15.3 us -> 0 us
  between operations: 13.7 us -> 0.01 us
  loops' own time: 5.33 us -> 0 us
    reduce_scatter x1 -> x0, waiting for transfers between devices: 244 us -> none  [per_device(): lax.psum_scatter(blocks.reshape(lax.axis_size('sub') * dm_dev, beams, out...]
    pallas_call x0 -> x2, Pallas kernels: none -> 40.4 us  [the longest x1 38.6 us: per_device(): pl.pallas_call(functools.partial(dedisperse_kernel, scale, blocks), out_s...]
    ppermute x2 -> x0, starting transfers between devices: 16.1 us -> none  [passed_along(): lax.ppermute(value, axis, [(source, source + steps) for source in range(i...]
    dot_general x25 -> x0, matrix products: 15.3 us -> none  [the longest x8 10.7 us: project(): jnp.einsum('msk,bskt->mbt', onehot, hankel, preferred_element_type=jnp.fl...]
    all_to_all x1 -> x0, starting transfers between devices: 11 us -> none  [per_device(): lax.all_to_all(offsets, 'sub', split_axis=1, concat_axis=0, tiled=True)]
    unnamed x102 -> x0, local copies, waits for them, and re-layouts: 10.9 us -> none
    another operation x1 -> x0, loops' own time: 5.33 us -> none  [per_device(): lax.map(one_block, jnp.arange(lax.axis_size('sub') * dm_dev // block, dty...]
    dynamic_slice x16 -> x0, local copies, waits for them, and re-layouts: 4.73 us -> none  [the longest x8 4.66 us: per_device(): lax.map(one_block, jnp.arange(lax.axis_size('sub') * dm_dev // block, dty...]
  transfers between devices with their start and end apart: 4 -> 0, of which waited for: 2 -> 0; matrix products, arithmetic and copies ran while one was open for 5% -> 0% of each run, Pallas kernels for 0% -> 0%
where the time goes in v1:
time: 40.6 us; the launch traced here: 40.4 us
  Pallas kernels  40.4 us (100%)
    pallas_call x1, Pallas kernels, per_device(): pl.pallas_call(functools.partial(dedisperse_kernel, scale, blocks), out_s...  38.6 us
    pallas_call x1, Pallas kernels, per_device(): pl.pallas_call(boxcar_kernel, out_shape=jax.ShapeDtypeStruct((dms * count...  1.87 us

profile of v1, /device:TPU:1, one launch (start us, length us, event | category | flops | bytes accessed | tf_op | source)
XLA Modules:
  0.0 40.4 jit_solution(1005524214738622467)
XLA Ops:
  0.0 38.6 %shard_map.46.series_ref = bf16[32,384]{1,0:T(8,128)(2,1)} custom-call(bf16[256,256]{1,0:T(8,128)(2,1)} %bitcast.5, s32[1,256]{1,0:T(1,128)} %bitcast.6, s32[32,1024]{1,0:T(8,128)} %offsets_ref.1), custom_call_target="tpu_custom_call" | custom-call | tf_op jit(solution)/shard_map/pallas_call | solution.py:287
  38.6 1.9 %shard_map.47 = f32[256,256]{1,0:T(8,128)} custom-call(s32[8]{0:T(128)} %widths_ref.1, bf16[32,384]{1,0:T(8,128)(2,1)} %shard_map.46.series_ref), custom_call_target="tpu_custom_call" | custom-call | tf_op jit(solution)/shard_map/pallas_call | solution.py:306

commit v2 on v1

--- a/solution.py
+++ b/solution.py
@@ -14,7 +14,7 @@
 RING = 8
 LANES = 128
 EDGE = 112
-STEP = 8
+STEP = 97
 MESH = pl.DeviceIdType.MESH
 FAR_FIRST = (4, 3, 5, 2, 6, 1, 7)
 NEAR_FIRST = (1, 7, 2, 6, 3, 5, 4)
@@ -36,7 +36,7 @@
     own_buf,
     halo_out,
     halo_buf,
-    series_buf,
+    turned,
     part_buf,
     sum_buf,
     send_own,
@@ -169,29 +169,30 @@
     own = own_buf[...].reshape(rows, length)
     halo = halo_buf[...].reshape(rows, LANES)
     edge = jnp.where(iota((rows, LANES), 1) >= EDGE, halo.astype(jnp.float32), 0.0)
-    tail = (own[:, length - LANES :].astype(jnp.float32) + edge).astype(jnp.bfloat16)
-    series_buf[...] = jnp.concatenate([own[:, : length - LANES], tail, halo], axis=1)
-
-    table = lags[...].reshape(RING * dms, rows)
+    tail = own[:, length - LANES :].astype(jnp.float32) + edge
+    tail = tail.astype(jnp.bfloat16).astype(jnp.float32)
+    body = own[:, : length - LANES].astype(jnp.float32)
+    turned[...] = jnp.concatenate([body, tail, halo.astype(jnp.float32)], axis=1).T
+
+    table = lags[...].reshape(RING * dms, rows).astype(jnp.float32).T.astype(jnp.bfloat16)
 
     def some_lags(block, total):
         base = block * STEP
-        here = pltpu.roll(series_buf[...], wide - base, 1)
         masks, windows = [], []
         for j in range(STEP):
             lag = (base + j).astype(jnp.float32).astype(jnp.bfloat16)
             masks.append(jnp.where(table == lag, jnp.bfloat16(1), jnp.bfloat16(0)))
-            windows.append(here[:, j : j + length])
+            windows.append(turned[pl.ds(base + j, length), :].astype(jnp.bfloat16))
         return total + jnp.dot(
-            jnp.concatenate(masks, axis=1),
-            jnp.concatenate(windows, axis=0),
+            jnp.concatenate(windows, axis=1),
+            jnp.concatenate(masks, axis=0),
             preferred_element_type=jnp.float32,
         )
 
     total = lax.fori_loop(
-        0, pl.cdiv(OMAX + 1, STEP), some_lags, jnp.zeros((RING * dms, length), jnp.float32)
-    )
-    part_buf[...] = total.astype(jnp.bfloat16).reshape(RING, dms, length)
+        0, pl.cdiv(OMAX + 1, STEP), some_lags, jnp.zeros((length, RING * dms), jnp.float32)
+    )
+    part_buf[...] = total.T.astype(jnp.bfloat16).reshape(RING, dms, length)
 
     def part_copy(d, source):
         g = lax.rem(z + d, RING)
@@ -295,7 +296,7 @@
                 pltpu.VMEM((RING, per, length), bf16),
                 pltpu.VMEM((per, LANES), bf16),
                 pltpu.VMEM((RING, per, LANES), bf16),
-                pltpu.VMEM((RING * per, length + LANES), bf16),
+                pltpu.VMEM((length + LANES, RING * per), jnp.float32),
                 pltpu.VMEM((RING, dms, length), bf16),
                 pltpu.VMEM((RING, dms, length + LANES), bf16),
             ]

time: 40.6 us -> 35.4 us (0.87)
  Pallas kernels: 40.4 us -> 35.2 us
    pallas_call x1, Pallas kernels: 38.6 us -> 33.3 us  [per_device(): pl.pallas_call(functools.partial(dedisperse_kernel, scale, blocks), out_s...]
where the time goes in v2:
time: 35.4 us; the launch traced here: 35.2 us
  Pallas kernels  35.2 us (99%)
    pallas_call x1, Pallas kernels, per_device(): pl.pallas_call(functools.partial(dedisperse_kernel, scale, blocks), out_s...  33.3 us
    pallas_call x1, Pallas kernels, per_device(): pl.pallas_call(boxcar_kernel, out_shape=jax.ShapeDtypeStruct((dms * count...  1.87 us

profile of v2, /device:TPU:1, one launch (start us, length us, event | category | flops | bytes accessed | tf_op | source)
XLA Modules:
  0.0 35.2 jit_solution(7466724933883622417)
XLA Ops:
  0.0 33.3 %shard_map.46.series_ref = bf16[32,384]{1,0:T(8,128)(2,1)} custom-call(bf16[256,256]{1,0:T(8,128)(2,1)} %bitcast.5, s32[1,256]{1,0:T(1,128)} %bitcast.6, s32[32,1024]{1,0:T(8,128)} %offsets_ref.1), custom_call_target="tpu_custom_call" | custom-call | tf_op jit(solution)/shard_map/pallas_call | solution.py:288
  33.4 1.9 %shard_map.47 = f32[256,256]{1,0:T(8,128)} custom-call(s32[8]{0:T(128)} %widths_ref.1, bf16[32,384]{1,0:T(8,128)(2,1)} %shard_map.46.series_ref), custom_call_target="tpu_custom_call" | custom-call | tf_op jit(solution)/shard_map/pallas_call | solution.py:307

commit v3 on v2

--- a/solution.py
+++ b/solution.py
@@ -27,10 +27,13 @@
 def dedisperse_kernel(
     scale,
     blocks,
+    data_hbm,
+    delays_hbm,
+    offsets_hbm,
+    out_ref,
     data_ref,
     delays_ref,
     offsets_ref,
-    out_ref,
     lag_out,
     lags,
     own_buf,
@@ -49,6 +52,7 @@
     recv_part,
     send_edge,
     recv_edge,
+    load,
 ):
     sub = lax.axis_index("sub")
     tm = lax.axis_index("tm")
@@ -66,26 +70,33 @@
 
     barrier = pltpu.get_barrier_semaphore()
 
+    def fetch(i, source, target):
+        return pltpu.make_async_copy(source, target, load.at[i])
+
+    fetch(0, data_hbm, data_ref).start()
+    fetch(1, delays_hbm, delays_ref).start()
+    fetch(2, offsets_hbm, offsets_ref).start()
+
     def greet(block, with_self):
-        for d in range(0 if with_self else 1, RING):
+        for d in FAR_FIRST:
             pl.semaphore_signal(barrier, inc=1, device_id=(along_y(d), block), device_id_type=MESH)
-        for d in range(1, RING):
             pl.semaphore_signal(barrier, inc=1, device_id=(along_z(d), block), device_id_type=MESH)
+        if with_self:
+            pl.semaphore_signal(barrier, inc=1, device_id=(along_y(0), block), device_id_type=MESH)
 
     greet(tm, False)
 
-    @pl.when(tm > 0)
-    def _():
-        greet(tm - 1, True)
-
     @pl.when(tm < blocks - 1)
     def _():
         greet(tm + 1, True)
 
+    fetch(2, offsets_hbm, offsets_ref).wait()
     for g in range(RING):
         lag_out[g] = offsets_ref[:, g * LANES : (g + 1) * LANES].astype(jnp.float32).astype(jnp.bfloat16)
     lags[z] = lag_out[z]
 
+    fetch(0, data_hbm, data_ref).wait()
+    fetch(1, delays_hbm, delays_ref).wait()
     eye = iota((chans, chans), 0) == iota((chans, chans), 1)
     diagonal = jnp.where(eye, delays_ref[...], 0).astype(jnp.float32).astype(jnp.bfloat16)
     delay = jnp.dot(diagonal, jnp.ones((chans, LANES), jnp.bfloat16), preferred_element_type=jnp.float32)
@@ -108,8 +119,7 @@
 
     pl.semaphore_wait(
         barrier,
-        2 * (RING - 1)
-        + (2 * RING - 1) * (jnp.where(first, 0, 1) + jnp.where(last, 0, 1)),
+        2 * (RING - 1) + jnp.where(first, 0, 2 * RING - 1),
     )
 
     def lag_copy(d, source):
@@ -256,20 +266,22 @@
 
 
 def boxcar_kernel(widths_ref, series_ref, out_ref, woven):
-    span = series_ref.shape[1]
     length = out_ref.shape[1]
     count = widths_ref.shape[0]
     dms = series_ref.shape[0]
-    lag = iota((span, length), 0) - iota((span, length), 1)
+    tiles = length // LANES
+    spans = [series_ref[:, h * LANES : (h + 2) * LANES] for h in range(tiles)]
+    spans = jnp.concatenate(spans, axis=0)
+    lag = iota((2 * LANES, LANES), 0) - iota((2 * LANES, LANES), 1)
+    lag = jnp.where(lag < 0, WMAX, lag)
     for i in range(count):
         width = widths_ref[i]
-        window = jnp.where((lag >= 0) & (lag < width), 1.0, 0.0).astype(jnp.bfloat16)
-        total = jnp.dot(series_ref[...], window, preferred_element_type=jnp.float32)
-        root = jnp.sqrt(jnp.full((dms, length), width, jnp.int32).astype(jnp.float32))
-        total = total / root
-        for h in range(length // LANES):
-            woven[h, pl.ds(i, dms, stride=count), :] = total[:, h * LANES : (h + 1) * LANES]
-    for h in range(length // LANES):
+        window = jnp.where(lag < width, 1.0, 0.0).astype(jnp.bfloat16)
+        total = jnp.dot(spans, window, preferred_element_type=jnp.float32)
+        total = total / jnp.sqrt(jnp.full((1, LANES), width, jnp.int32).astype(jnp.float32))
+        for h in range(tiles):
+            woven[h, pl.ds(i, dms, stride=count), :] = total[h * dms : (h + 1) * dms]
+    for h in range(tiles):
         out_ref[:, h * LANES : (h + 1) * LANES] = woven[h]
 
 
@@ -288,9 +300,12 @@
         series = pl.pallas_call(
             functools.partial(dedisperse_kernel, scale, blocks),
             out_shape=jax.ShapeDtypeStruct((dms, length + LANES), bf16),
-            in_specs=[vmem] * 3,
+            in_specs=[pl.BlockSpec(memory_space=pl.ANY)] * 3,
             out_specs=vmem,
             scratch_shapes=[
+                pltpu.VMEM((chans, length), bf16),
+                pltpu.VMEM((1, chans), jnp.int32),
+                pltpu.VMEM((dms, nsub), jnp.int32),
                 pltpu.VMEM((RING, dms, LANES), bf16),
                 pltpu.VMEM((RING, dms, LANES), bf16),
                 pltpu.VMEM((RING, per, length), bf16),
@@ -300,7 +315,8 @@
                 pltpu.VMEM((RING, dms, length), bf16),
                 pltpu.VMEM((RING, dms, length + LANES), bf16),
             ]
-            + [dma] * 10,
+            + [dma] * 10
+            + [pltpu.SemaphoreType.DMA((3,))],
             compiler_params=pltpu.CompilerParams(collective_id=0, has_side_effects=True),
         )(data[0], delays[None, :], offsets)
         count = widths.shape[0]

time: 35.4 us -> 31.7 us (0.90)
  Pallas kernels: 35.2 us -> 31.5 us
    pallas_call x1, Pallas kernels: 33.3 us -> 29.8 us  [per_device(): pl.pallas_call(functools.partial(dedisperse_kernel, scale, blocks), out_s...]
where the time goes in v3:
time: 31.7 us; the launch traced here: 31.5 us
  Pallas kernels  31.5 us (99%)
    pallas_call x1, Pallas kernels, per_device(): pl.pallas_call(functools.partial(dedisperse_kernel, scale, blocks), out_s...  29.8 us
    pallas_call x1, Pallas kernels, per_device(): pl.pallas_call(boxcar_kernel, out_shape=jax.ShapeDtypeStruct((dms * count...  1.71 us

profile of v3, /device:TPU:1, one launch (start us, length us, event | category | flops | bytes accessed | tf_op | source)
XLA Modules:
  0.0 31.5 jit_solution(2324495444877638083)
XLA Ops:
  0.0 29.8 %shard_map.46.series_ref = bf16[32,384]{1,0:T(8,128)(2,1)} custom-call(bf16[256,256]{1,0:T(8,128)(2,1)} %bitcast.5, s32[1,256]{1,0:T(1,128)} %bitcast.6, s32[32,1024]{1,0:T(8,128)} %offsets_hbm.1), custom_call_target="tpu_custom_call" | custom-call | tf_op jit(solution)/shard_map/pallas_call | solution.py:300
  29.8 1.7 %shard_map.47 = f32[256,256]{1,0:T(8,128)} custom-call(s32[8]{0:T(128)} %widths_ref.1, bf16[32,384]{1,0:T(8,128)(2,1)} %shard_map.46.series_ref), custom_call_target="tpu_custom_call" | custom-call | tf_op jit(solution)/shard_map/pallas_call | solution.py:323

commit v4 on v3

--- a/solution.py
+++ b/solution.py
@@ -14,7 +14,6 @@
 RING = 8
 LANES = 128
 EDGE = 112
-STEP = 97
 MESH = pl.DeviceIdType.MESH
 FAR_FIRST = (4, 3, 5, 2, 6, 1, 7)
 NEAR_FIRST = (1, 7, 2, 6, 3, 5, 4)
@@ -42,6 +41,8 @@
     turned,
     part_buf,
     sum_buf,
+    edge_out,
+    edge_in,
     send_own,
     recv_own,
     send_halo,
@@ -77,18 +78,14 @@
     fetch(1, delays_hbm, delays_ref).start()
     fetch(2, offsets_hbm, offsets_ref).start()
 
-    def greet(block, with_self):
-        for d in FAR_FIRST:
-            pl.semaphore_signal(barrier, inc=1, device_id=(along_y(d), block), device_id_type=MESH)
-            pl.semaphore_signal(barrier, inc=1, device_id=(along_z(d), block), device_id_type=MESH)
-        if with_self:
-            pl.semaphore_signal(barrier, inc=1, device_id=(along_y(0), block), device_id_type=MESH)
-
-    greet(tm, False)
-
-    @pl.when(tm < blocks - 1)
-    def _():
-        greet(tm + 1, True)
+    for d in FAR_FIRST:
+        pl.semaphore_signal(barrier, inc=1, device_id=(along_y(d), tm), device_id_type=MESH)
+        pl.semaphore_signal(barrier, inc=1, device_id=(along_z(d), tm), device_id_type=MESH)
+
+    @pl.when(jnp.logical_not(last))
+    def _():
+        for d in FAR_FIRST + (0,):
+            pl.semaphore_signal(barrier, inc=1, device_id=(along_y(d), tm + 1), device_id_type=MESH)
 
     fetch(2, offsets_hbm, offsets_ref).wait()
     for g in range(RING):
@@ -119,7 +116,7 @@
 
     pl.semaphore_wait(
         barrier,
-        2 * (RING - 1) + jnp.where(first, 0, 2 * RING - 1),
+        2 * (RING - 1) + jnp.where(first, 0, RING),
     )
 
     def lag_copy(d, source):
@@ -170,99 +167,105 @@
         lag_copy(d, lax.rem(z + d, RING)).wait_recv()
         own_copy(d, lax.rem(y + d, RING)).wait_recv()
 
-    @pl.when(jnp.logical_not(last))
-    def _():
-        for d in (0,) + NEAR_FIRST:
-            halo_copy(d, lax.rem(y + d, RING)).wait_recv()
-
     rows = RING * per
-    own = own_buf[...].reshape(rows, length)
-    halo = halo_buf[...].reshape(rows, LANES)
-    edge = jnp.where(iota((rows, LANES), 1) >= EDGE, halo.astype(jnp.float32), 0.0)
-    tail = own[:, length - LANES :].astype(jnp.float32) + edge
-    tail = tail.astype(jnp.bfloat16).astype(jnp.float32)
-    body = own[:, : length - LANES].astype(jnp.float32)
-    turned[...] = jnp.concatenate([body, tail, halo.astype(jnp.float32)], axis=1).T
+    turned[:length] = own_buf[...].reshape(rows, length).astype(jnp.float32).T
 
     table = lags[...].reshape(RING * dms, rows).astype(jnp.float32).T.astype(jnp.bfloat16)
 
-    def some_lags(block, total):
-        base = block * STEP
+    def part_copy(t, d, source):
+        return pltpu.make_async_remote_copy(
+            src_ref=part_buf.at[t, lax.rem(z + d, RING)],
+            dst_ref=sum_buf.at[t, source],
+            send_sem=send_part.at[t * RING + d],
+            recv_sem=recv_part.at[t * RING + source],
+            device_id=(along_z(d), tm),
+            device_id_type=MESH,
+        )
+
+    def edge_copy():
+        return pltpu.make_async_remote_copy(
+            src_ref=edge_out,
+            dst_ref=edge_in,
+            send_sem=send_edge.at[0],
+            recv_sem=recv_edge.at[0],
+            device_id=(sub, tm - 1),
+            device_id_type=MESH,
+        )
+
+    def add_halo():
+        @pl.when(jnp.logical_not(last))
+        def _():
+            for d in (0,) + NEAR_FIRST:
+                halo_copy(d, lax.rem(y + d, RING)).wait_recv()
+
+        halo = halo_buf[...].reshape(rows, LANES).astype(jnp.float32)
+        edge = jnp.where(iota((rows, LANES), 1) >= EDGE, halo, 0.0)
+        tail = own_buf[:, :, length - LANES :].reshape(rows, LANES).astype(jnp.float32) + edge
+        turned[length - LANES : length] = tail.astype(jnp.bfloat16).astype(jnp.float32).T
+        turned[length:] = halo.T
+
+    tiles = length // LANES
+
+    def tile(t, carry):
+        pl.when(t == tiles - 1)(add_halo)
         masks, windows = [], []
-        for j in range(STEP):
-            lag = (base + j).astype(jnp.float32).astype(jnp.bfloat16)
-            masks.append(jnp.where(table == lag, jnp.bfloat16(1), jnp.bfloat16(0)))
-            windows.append(turned[pl.ds(base + j, length), :].astype(jnp.bfloat16))
-        return total + jnp.dot(
+        for j in range(OMAX + 1):
+            masks.append(jnp.where(table == jnp.bfloat16(j), jnp.bfloat16(1), jnp.bfloat16(0)))
+            windows.append(turned[pl.ds(t * LANES + j, LANES), :].astype(jnp.bfloat16))
+        total = jnp.dot(
             jnp.concatenate(windows, axis=1),
             jnp.concatenate(masks, axis=0),
             preferred_element_type=jnp.float32,
         )
-
-    total = lax.fori_loop(
-        0, pl.cdiv(OMAX + 1, STEP), some_lags, jnp.zeros((length, RING * dms), jnp.float32)
-    )
-    part_buf[...] = total.T.astype(jnp.bfloat16).reshape(RING, dms, length)
-
-    def part_copy(d, source):
-        g = lax.rem(z + d, RING)
-        return pltpu.make_async_remote_copy(
-            src_ref=part_buf.at[g],
-            dst_ref=sum_buf.at[source, :, pl.ds(0, length)],
-            send_sem=send_part.at[d],
-            recv_sem=recv_part.at[source],
-            device_id=(along_z(d), tm),
-            device_id_type=MESH,
-        )
-
-    def edge_copy(d, source):
-        g = lax.rem(z + d, RING)
-        return pltpu.make_async_remote_copy(
-            src_ref=part_buf.at[g, :, pl.ds(0, LANES)],
-            dst_ref=sum_buf.at[source, :, pl.ds(length, LANES)],
-            send_sem=send_edge.at[d],
-            recv_sem=recv_edge.at[source],
-            device_id=(along_z(d), tm - 1),
-            device_id_type=MESH,
-        )
-
-    for d in FAR_FIRST:
-        part_copy(d, z).start()
+        part_buf[t] = total.T.astype(jnp.bfloat16).reshape(RING, dms, LANES)
+        for d in FAR_FIRST:
+            part_copy(t, d, z).start()
+
+        sum_buf[t, z] = part_buf[t, z]
+        return carry
+
+    lax.fori_loop(0, tiles, tile, 0)
+
+    def finish(t):
+        for d in NEAR_FIRST:
+            part_copy(t, d, lax.rem(z + d, RING)).wait_recv()
+        added = sum_buf[t, 0].astype(jnp.float32)
+        for g in range(1, RING):
+            added = added + sum_buf[t, g].astype(jnp.float32)
+        return (added * scale).astype(jnp.bfloat16)
+
+    start = finish(0)
+    edge_out[...] = start
 
     @pl.when(tm > 0)
     def _():
-        for d in FAR_FIRST + (0,):
-            edge_copy(d, z).start()
+        edge_copy().start()
+
+    out_ref[:, :LANES] = start
+    for t in range(1, tiles):
+        out_ref[:, t * LANES : (t + 1) * LANES] = finish(t)
 
     @pl.when(last)
     def _():
-        sum_buf[:, :, length:] = jnp.zeros((RING, dms, LANES), jnp.bfloat16)
-
-    sum_buf[z, :, :length] = part_buf[z]
-
-    for d in NEAR_FIRST:
-        part_copy(d, lax.rem(z + d, RING)).wait_recv()
+        edge_in[...] = jnp.zeros((dms, LANES), jnp.bfloat16)
 
     @pl.when(jnp.logical_not(last))
     def _():
-        for d in (0,) + NEAR_FIRST:
-            edge_copy(d, lax.rem(z + d, RING)).wait_recv()
-
-    added = sum_buf[0].astype(jnp.float32)
-    for g in range(1, RING):
-        added = added + sum_buf[g].astype(jnp.float32)
-    out_ref[...] = (added * scale).astype(jnp.bfloat16)
+        edge_copy().wait_recv()
+
+    out_ref[:, length:] = edge_in[...]
 
     for d in NEAR_FIRST:
         own_copy(d, y).wait_send()
         lag_copy(d, z).wait_send()
-        part_copy(d, z).wait_send()
+        for t in range(tiles):
+            part_copy(t, d, z).wait_send()
 
     @pl.when(tm > 0)
     def _():
         for d in (0,) + NEAR_FIRST:
             halo_copy(d, y).wait_send()
-            edge_copy(d, z).wait_send()
+        edge_copy().wait_send()
 
 
 def boxcar_kernel(widths_ref, series_ref, out_ref, woven):
@@ -312,10 +315,14 @@
                 pltpu.VMEM((per, LANES), bf16),
                 pltpu.VMEM((RING, per, LANES), bf16),
                 pltpu.VMEM((length + LANES, RING * per), jnp.float32),
-                pltpu.VMEM((RING, dms, length), bf16),
-                pltpu.VMEM((RING, dms, length + LANES), bf16),
+                pltpu.VMEM((length // LANES, RING, dms, LANES), bf16),
+                pltpu.VMEM((length // LANES, RING, dms, LANES), bf16),
+                pltpu.VMEM((dms, LANES), bf16),
+                pltpu.VMEM((dms, LANES), bf16),
             ]
-            + [dma] * 10
+            + [dma] * 6
+            + [pltpu.SemaphoreType.DMA((RING * (length // LANES),))] * 2
+            + [pltpu.SemaphoreType.DMA((1,))] * 2
             + [pltpu.SemaphoreType.DMA((3,))],
             compiler_params=pltpu.CompilerParams(collective_id=0, has_side_effects=True),
         )(data[0], delays[None, :], offsets)

time: 31.7 us -> 31.1 us (0.981)
  Pallas kernels: 31.5 us -> 30.9 us
    pallas_call x1, Pallas kernels: 29.8 us -> 29.2 us  [per_device(): pl.pallas_call(functools.partial(dedisperse_kernel, scale, blocks), out_s...]
where the time goes in v4:
time: 31.1 us; the launch traced here: 30.9 us
  Pallas kernels  30.9 us (99%)
    pallas_call x1, Pallas kernels, per_device(): pl.pallas_call(functools.partial(dedisperse_kernel, scale, blocks), out_s...  29.2 us
    pallas_call x1, Pallas kernels, per_device(): pl.pallas_call(boxcar_kernel, out_shape=jax.ShapeDtypeStruct((dms * count...  1.71 us

profile of v4, /device:TPU:1, one launch (start us, length us, event | category | flops | bytes accessed | tf_op | source)
XLA Modules:
  0.0 30.9 jit_solution(941518472907816944)
XLA Ops:
  0.0 29.2 %shard_map.46.series_ref = bf16[32,384]{1,0:T(8,128)(2,1)} custom-call(bf16[256,256]{1,0:T(8,128)(2,1)} %bitcast.5, s32[1,256]{1,0:T(1,128)} %bitcast.6, s32[32,1024]{1,0:T(8,128)} %offsets_hbm.1), custom_call_target="tpu_custom_call" | custom-call | tf_op jit(solution)/shard_map/pallas_call | solution.py:303
  29.2 1.7 %shard_map.47 = f32[256,256]{1,0:T(8,128)} custom-call(s32[8]{0:T(128)} %widths_ref.1, bf16[32,384]{1,0:T(8,128)(2,1)} %shard_map.46.series_ref), custom_call_target="tpu_custom_call" | custom-call | tf_op jit(solution)/shard_map/pallas_call | solution.py:330

commit v5 on v4

--- a/solution.py
+++ b/solution.py
@@ -94,21 +94,16 @@
 
     fetch(0, data_hbm, data_ref).wait()
     fetch(1, delays_hbm, delays_ref).wait()
-    eye = iota((chans, chans), 0) == iota((chans, chans), 1)
-    diagonal = jnp.where(eye, delays_ref[...], 0).astype(jnp.float32).astype(jnp.bfloat16)
-    delay = jnp.dot(diagonal, jnp.ones((chans, LANES), jnp.bfloat16), preferred_element_type=jnp.float32)
-    delay = delay.astype(jnp.int32)
-    delay = jnp.concatenate([delay] * 3, axis=1)
+    pick, chan = iota((DCH * per, chans), 0), iota((DCH * per, chans), 1)
+    same = jnp.logical_and(chan // (chans // per) == pick % per, delays_ref[...] == pick // per)
+    spread = jnp.dot(
+        jnp.where(same, 1.0, 0.0).astype(jnp.bfloat16), data_ref[...], preferred_element_type=jnp.float32
+    )
     wide = length + LANES
-    moved = jnp.concatenate(
-        [jnp.zeros((chans, LANES), jnp.float32), data_ref[...].astype(jnp.float32)], axis=1
-    )
-    for bit in (1, 2, 4, 8):
-        moved = jnp.where((delay & bit) != 0, pltpu.roll(moved, wide - bit, 1), moved)
-    member = (iota((per, chans), 1) // (chans // per) == iota((per, chans), 0)).astype(jnp.float32)
-    summed = jnp.dot(
-        member.astype(jnp.bfloat16), moved.astype(jnp.bfloat16), preferred_element_type=jnp.float32
-    )
+    summed = jnp.zeros((per, wide), jnp.float32)
+    for j in range(DCH):
+        part = jnp.concatenate([jnp.zeros((per, LANES), jnp.float32), spread[j * per : (j + 1) * per]], axis=1)
+        summed = summed + (pltpu.roll(part, wide - j, 1) if j else part)
     own_buf[y] = summed[:, LANES:].astype(jnp.bfloat16)
     halo_out[...] = jnp.where(
         iota((per, LANES), 1) < EDGE, summed[:, LANES : 2 * LANES], summed[:, :LANES]

time: 31.1 us -> 31.2 us (level)
  no operation moved by 1% of the time
where the time goes in v5:
time: 31.2 us; the launch traced here: 31 us
  Pallas kernels  31 us (99%)
    pallas_call x1, Pallas kernels, per_device(): pl.pallas_call(functools.partial(dedisperse_kernel, scale, blocks), out_s...  29.3 us
    pallas_call x1, Pallas kernels, per_device(): pl.pallas_call(boxcar_kernel, out_shape=jax.ShapeDtypeStruct((dms * count...  1.7 us

profile of v5, /device:TPU:1, one launch (start us, length us, event | category | flops | bytes accessed | tf_op | source)
XLA Modules:
  0.0 31.0 jit_solution(11206344945319525708)
XLA Ops:
  0.0 29.3 %shard_map.46.series_ref = bf16[32,384]{1,0:T(8,128)(2,1)} custom-call(bf16[256,256]{1,0:T(8,128)(2,1)} %bitcast.5, s32[1,256]{1,0:T(1,128)} %bitcast.6, s32[32,1024]{1,0:T(8,128)} %offsets_hbm.1), custom_call_target="tpu_custom_call" | custom-call | tf_op jit(solution)/shard_map/pallas_call | solution.py:298
  29.3 1.7 %shard_map.47 = f32[256,256]{1,0:T(8,128)} custom-call(s32[8]{0:T(128)} %widths_ref.1, bf16[32,384]{1,0:T(8,128)(2,1)} %shard_map.46.series_ref), custom_call_target="tpu_custom_call" | custom-call | tf_op jit(solution)/shard_map/pallas_call | solution.py:325

commit v6 on v5

--- a/solution.py
+++ b/solution.py
@@ -84,8 +84,7 @@
 
     @pl.when(jnp.logical_not(last))
     def _():
-        for d in FAR_FIRST + (0,):
-            pl.semaphore_signal(barrier, inc=1, device_id=(along_y(d), tm + 1), device_id_type=MESH)
+        pl.semaphore_signal(barrier, inc=1, device_id=(sub, tm + 1), device_id_type=MESH)
 
     fetch(2, offsets_hbm, offsets_ref).wait()
     for g in range(RING):
@@ -109,10 +108,7 @@
         iota((per, LANES), 1) < EDGE, summed[:, LANES : 2 * LANES], summed[:, :LANES]
     ).astype(jnp.bfloat16)
 
-    pl.semaphore_wait(
-        barrier,
-        2 * (RING - 1) + jnp.where(first, 0, RING),
-    )
+    pl.semaphore_wait(barrier, 2 * (RING - 1) + jnp.where(first, 0, 1))
 
     def lag_copy(d, source):
         g = lax.rem(z + d, RING)
@@ -135,37 +131,52 @@
             device_id_type=MESH,
         )
 
+    def hop_copy():
+        return pltpu.make_async_remote_copy(
+            src_ref=halo_out,
+            dst_ref=halo_buf.at[y],
+            send_sem=send_edge.at[1],
+            recv_sem=recv_edge.at[1],
+            device_id=(sub, tm - 1),
+            device_id_type=MESH,
+        )
+
     def halo_copy(d, source):
         return pltpu.make_async_remote_copy(
-            src_ref=halo_out,
+            src_ref=halo_buf.at[y],
             dst_ref=halo_buf.at[source],
             send_sem=send_halo.at[d],
             recv_sem=recv_halo.at[source],
-            device_id=(along_y(d), tm - 1),
-            device_id_type=MESH,
-        )
+            device_id=(along_y(d), tm),
+            device_id_type=MESH,
+        )
+
+    @pl.when(tm > 0)
+    def _():
+        hop_copy().start()
 
     for d in FAR_FIRST:
         own_copy(d, y).start()
         lag_copy(d, z).start()
 
-    @pl.when(tm > 0)
-    def _():
-        for d in FAR_FIRST + (0,):
+    @pl.when(last)
+    def _():
+        halo_buf[...] = jnp.zeros(halo_buf.shape, halo_buf.dtype)
+
+    @pl.when(jnp.logical_not(last))
+    def _():
+        hop_copy().wait_recv()
+        for d in FAR_FIRST:
             halo_copy(d, y).start()
 
-    @pl.when(last)
-    def _():
-        halo_buf[...] = jnp.zeros(halo_buf.shape, halo_buf.dtype)
-
+    rows = RING * per
     for d in NEAR_FIRST:
         lag_copy(d, lax.rem(z + d, RING)).wait_recv()
+    table = lags[...].reshape(RING * dms, rows).astype(jnp.float32).T.astype(jnp.bfloat16)
+
+    for d in NEAR_FIRST:
         own_copy(d, lax.rem(y + d, RING)).wait_recv()
-
-    rows = RING * per
     turned[:length] = own_buf[...].reshape(rows, length).astype(jnp.float32).T
-
-    table = lags[...].reshape(RING * dms, rows).astype(jnp.float32).T.astype(jnp.bfloat16)
 
     def part_copy(t, d, source):
         return pltpu.make_async_remote_copy(
@@ -190,7 +201,7 @@
     def add_halo():
         @pl.when(jnp.logical_not(last))
         def _():
-            for d in (0,) + NEAR_FIRST:
+            for d in NEAR_FIRST:
                 halo_copy(d, lax.rem(y + d, RING)).wait_recv()
 
         halo = halo_buf[...].reshape(rows, LANES).astype(jnp.float32)
@@ -256,10 +267,14 @@
         for t in range(tiles):
             part_copy(t, d, z).wait_send()
 
+    @pl.when(jnp.logical_not(last))
+    def _():
+        for d in NEAR_FIRST:
+            halo_copy(d, y).wait_send()
+
     @pl.when(tm > 0)
     def _():
-        for d in (0,) + NEAR_FIRST:
-            halo_copy(d, y).wait_send()
+        hop_copy().wait_send()
         edge_copy().wait_send()
 
 
@@ -317,7 +332,7 @@
             ]
             + [dma] * 6
             + [pltpu.SemaphoreType.DMA((RING * (length // LANES),))] * 2
-            + [pltpu.SemaphoreType.DMA((1,))] * 2
+            + [pltpu.SemaphoreType.DMA((2,))] * 2
             + [pltpu.SemaphoreType.DMA((3,))],
             compiler_params=pltpu.CompilerParams(collective_id=0, has_side_effects=True),
         )(data[0], delays[None, :], offsets)

time: 31.2 us -> 30.8 us (0.987)
  Pallas kernels: 31 us -> 30.6 us
    pallas_call x1, Pallas kernels: 29.3 us -> 28.9 us  [per_device(): pl.pallas_call(functools.partial(dedisperse_kernel, scale, blocks), out_s...]
where the time goes in v6:
time: 30.8 us; the launch traced here: 30.7 us
  Pallas kernels  30.6 us (99%)
    pallas_call x1, Pallas kernels, per_device(): pl.pallas_call(functools.partial(dedisperse_kernel, scale, blocks), out_s...  28.9 us
    pallas_call x1, Pallas kernels, per_device(): pl.pallas_call(boxcar_kernel, out_shape=jax.ShapeDtypeStruct((dms * count...  1.71 us

profile of v6, /device:TPU:1, one launch (start us, length us, event | category | flops | bytes accessed | tf_op | source)
XLA Modules:
  0.0 30.7 jit_solution(6188838167907653334)
XLA Ops:
  0.0 28.9 %shard_map.46.series_ref = bf16[32,384]{1,0:T(8,128)(2,1)} custom-call(bf16[256,256]{1,0:T(8,128)(2,1)} %bitcast.5, s32[1,256]{1,0:T(1,128)} %bitcast.6, s32[32,1024]{1,0:T(8,128)} %offsets_hbm.1), custom_call_target="tpu_custom_call" | custom-call | tf_op jit(solution)/shard_map/pallas_call | solution.py:313
  29.0 1.7 %shard_map.47 = f32[256,256]{1,0:T(8,128)} custom-call(s32[8]{0:T(128)} %widths_ref.1, bf16[32,384]{1,0:T(8,128)(2,1)} %shard_map.46.series_ref), custom_call_target="tpu_custom_call" | custom-call | tf_op jit(solution)/shard_map/pallas_call | solution.py:340

commit v7 on v6

--- a/solution.py
+++ b/solution.py
@@ -17,6 +17,9 @@
 MESH = pl.DeviceIdType.MESH
 FAR_FIRST = (4, 3, 5, 2, 6, 1, 7)
 NEAR_FIRST = (1, 7, 2, 6, 3, 5, 4)
+NEAR = (2, 6, 1, 7)
+RELAYS = {3: (1, 2, 7), 5: (7, 6, 1), 4: (2, 2, 6)}
+LATE = (2, 3, 5, 4)
 
 
 def iota(shape, dim):
@@ -35,6 +38,7 @@
     offsets_ref,
     lag_out,
     lags,
+    passing,
     own_buf,
     halo_out,
     halo_buf,
@@ -49,6 +53,8 @@
     recv_halo,
     send_lag,
     recv_lag,
+    send_pass,
+    recv_pass,
     send_part,
     recv_part,
     send_edge,
@@ -78,7 +84,7 @@
     fetch(1, delays_hbm, delays_ref).start()
     fetch(2, offsets_hbm, offsets_ref).start()
 
-    for d in FAR_FIRST:
+    for d in NEAR:
         pl.semaphore_signal(barrier, inc=1, device_id=(along_y(d), tm), device_id_type=MESH)
         pl.semaphore_signal(barrier, inc=1, device_id=(along_z(d), tm), device_id_type=MESH)
 
@@ -108,7 +114,7 @@
         iota((per, LANES), 1) < EDGE, summed[:, LANES : 2 * LANES], summed[:, :LANES]
     ).astype(jnp.bfloat16)
 
-    pl.semaphore_wait(barrier, 2 * (RING - 1) + jnp.where(first, 0, 1))
+    pl.semaphore_wait(barrier, 2 * len(NEAR) + jnp.where(first, 0, 1))
 
     def lag_copy(d, source):
         g = lax.rem(z + d, RING)
@@ -121,13 +127,37 @@
             device_id_type=MESH,
         )
 
-    def own_copy(d, source):
-        return pltpu.make_async_remote_copy(
-            src_ref=own_buf.at[y],
+    def pass_copy(far):
+        step, _, _ = RELAYS[far]
+        return pltpu.make_async_remote_copy(
+            src_ref=lag_out.at[lax.rem(z + far, RING)],
+            dst_ref=passing.at[far - 3],
+            send_sem=send_lag.at[far],
+            recv_sem=recv_pass.at[far],
+            device_id=(along_z(step), tm),
+            device_id_type=MESH,
+        )
+
+    def onward_copy(far):
+        _, step, source = RELAYS[far]
+        source = lax.rem(z + source, RING)
+        return pltpu.make_async_remote_copy(
+            src_ref=passing.at[far - 3],
+            dst_ref=lags.at[source],
+            send_sem=send_pass.at[far],
+            recv_sem=recv_lag.at[source],
+            device_id=(along_z(step), tm),
+            device_id_type=MESH,
+        )
+
+    def own_copy(slot, step, source):
+        source = lax.rem(y + source, RING)
+        return pltpu.make_async_remote_copy(
+            src_ref=own_buf.at[source],
             dst_ref=own_buf.at[source],
-            send_sem=send_own.at[d],
+            send_sem=send_own.at[slot],
             recv_sem=recv_own.at[source],
-            device_id=(along_y(d), tm),
+            device_id=(along_y(step), tm),
             device_id_type=MESH,
         )
 
@@ -141,13 +171,14 @@
             device_id_type=MESH,
         )
 
-    def halo_copy(d, source):
-        return pltpu.make_async_remote_copy(
-            src_ref=halo_buf.at[y],
+    def halo_copy(slot, step, source):
+        source = lax.rem(y + source, RING)
+        return pltpu.make_async_remote_copy(
+            src_ref=halo_buf.at[source],
             dst_ref=halo_buf.at[source],
-            send_sem=send_halo.at[d],
+            send_sem=send_halo.at[slot],
             recv_sem=recv_halo.at[source],
-            device_id=(along_y(d), tm),
+            device_id=(along_y(step), tm),
             device_id_type=MESH,
         )
 
@@ -155,8 +186,10 @@
     def _():
         hop_copy().start()
 
-    for d in FAR_FIRST:
-        own_copy(d, y).start()
+    for far in RELAYS:
+        pass_copy(far).start()
+    for d in NEAR:
+        own_copy(d, d, 0).start()
         lag_copy(d, z).start()
 
     @pl.when(last)
@@ -166,16 +199,28 @@
     @pl.when(jnp.logical_not(last))
     def _():
         hop_copy().wait_recv()
-        for d in FAR_FIRST:
-            halo_copy(d, y).start()
+        for d in NEAR:
+            halo_copy(d, d, 0).start()
+
+    for far, (_, step, source) in RELAYS.items():
+        own_copy(far, step, source).wait_recv()
+        own_copy(far, step, source).start()
+        pass_copy(far).wait_recv()
+        onward_copy(far).start()
+
+    @pl.when(jnp.logical_not(last))
+    def _():
+        for far, (_, step, source) in RELAYS.items():
+            halo_copy(far, step, source).wait_recv()
+            halo_copy(far, step, source).start()
 
     rows = RING * per
     for d in NEAR_FIRST:
         lag_copy(d, lax.rem(z + d, RING)).wait_recv()
     table = lags[...].reshape(RING * dms, rows).astype(jnp.float32).T.astype(jnp.bfloat16)
 
-    for d in NEAR_FIRST:
-        own_copy(d, lax.rem(y + d, RING)).wait_recv()
+    for d in LATE:
+        own_copy(d, 1, d).wait_recv()
     turned[:length] = own_buf[...].reshape(rows, length).astype(jnp.float32).T
 
     def part_copy(t, d, source):
@@ -201,8 +246,8 @@
     def add_halo():
         @pl.when(jnp.logical_not(last))
         def _():
-            for d in NEAR_FIRST:
-                halo_copy(d, lax.rem(y + d, RING)).wait_recv()
+            for d in LATE:
+                halo_copy(d, 1, d).wait_recv()
 
         halo = halo_buf[...].reshape(rows, LANES).astype(jnp.float32)
         edge = jnp.where(iota((rows, LANES), 1) >= EDGE, halo, 0.0)
@@ -261,8 +306,10 @@
 
     out_ref[:, length:] = edge_in[...]
 
+    for far in RELAYS:
+        onward_copy(far).wait_send()
     for d in NEAR_FIRST:
-        own_copy(d, y).wait_send()
+        own_copy(d, 1, 0).wait_send()
         lag_copy(d, z).wait_send()
         for t in range(tiles):
             part_copy(t, d, z).wait_send()
@@ -270,7 +317,7 @@
     @pl.when(jnp.logical_not(last))
     def _():
         for d in NEAR_FIRST:
-            halo_copy(d, y).wait_send()
+            halo_copy(d, 1, 0).wait_send()
 
     @pl.when(tm > 0)
     def _():
@@ -321,6 +368,7 @@
                 pltpu.VMEM((dms, nsub), jnp.int32),
                 pltpu.VMEM((RING, dms, LANES), bf16),
                 pltpu.VMEM((RING, dms, LANES), bf16),
+                pltpu.VMEM((len(RELAYS), dms, LANES), bf16),
                 pltpu.VMEM((RING, per, length), bf16),
                 pltpu.VMEM((per, LANES), bf16),
                 pltpu.VMEM((RING, per, LANES), bf16),
@@ -330,7 +378,7 @@
                 pltpu.VMEM((dms, LANES), bf16),
                 pltpu.VMEM((dms, LANES), bf16),
             ]
-            + [dma] * 6
+            + [dma] * 8
             + [pltpu.SemaphoreType.DMA((RING * (length // LANES),))] * 2
             + [pltpu.SemaphoreType.DMA((2,))] * 2
             + [pltpu.SemaphoreType.DMA((3,))],

time: 30.8 us -> 32.5 us (1.055)
  Pallas kernels: 30.6 us -> 32.3 us
    pallas_call x1, Pallas kernels: 28.9 us -> 30.6 us  [per_device(): pl.pallas_call(functools.partial(dedisperse_kernel, scale, blocks), out_s...]
where the time goes in v7:
time: 32.5 us; the launch traced here: 32.3 us
  Pallas kernels  32.3 us (99%)
    pallas_call x1, Pallas kernels, per_device(): pl.pallas_call(functools.partial(dedisperse_kernel, scale, blocks), out_s...  30.6 us
    pallas_call x1, Pallas kernels, per_device(): pl.pallas_call(boxcar_kernel, out_shape=jax.ShapeDtypeStruct((dms * count...  1.71 us

profile of v7, /device:TPU:1, one launch (start us, length us, event | category | flops | bytes accessed | tf_op | source)
XLA Modules:
  0.0 32.3 jit_solution(8472832327134360249)
XLA Ops:
  0.0 30.6 %shard_map.46.series_ref = bf16[32,384]{1,0:T(8,128)(2,1)} custom-call(bf16[256,256]{1,0:T(8,128)(2,1)} %bitcast.5, s32[1,256]{1,0:T(1,128)} %bitcast.6, s32[32,1024]{1,0:T(8,128)} %offsets_hbm.1), custom_call_target="tpu_custom_call" | custom-call | tf_op jit(solution)/shard_map/pallas_call | solution.py:360
  30.6 1.7 %shard_map.47 = f32[256,256]{1,0:T(8,128)} custom-call(s32[8]{0:T(128)} %widths_ref.1, bf16[32,384]{1,0:T(8,128)(2,1)} %shard_map.46.series_ref), custom_call_target="tpu_custom_call" | custom-call | tf_op jit(solution)/shard_map/pallas_call | solution.py:388

commit v8 on v6

--- a/solution.py
+++ b/solution.py
@@ -37,7 +37,7 @@
     lags,
     own_buf,
     halo_out,
-    halo_buf,
+    halo_in,
     turned,
     part_buf,
     sum_buf,
@@ -45,8 +45,6 @@
     edge_in,
     send_own,
     recv_own,
-    send_halo,
-    recv_halo,
     send_lag,
     recv_lag,
     send_part,
@@ -103,7 +101,7 @@
     for j in range(DCH):
         part = jnp.concatenate([jnp.zeros((per, LANES), jnp.float32), spread[j * per : (j + 1) * per]], axis=1)
         summed = summed + (pltpu.roll(part, wide - j, 1) if j else part)
-    own_buf[y] = summed[:, LANES:].astype(jnp.bfloat16)
+    own_buf[y, :, :length] = summed[:, LANES:].astype(jnp.bfloat16)
     halo_out[...] = jnp.where(
         iota((per, LANES), 1) < EDGE, summed[:, LANES : 2 * LANES], summed[:, :LANES]
     ).astype(jnp.bfloat16)
@@ -134,40 +132,35 @@
     def hop_copy():
         return pltpu.make_async_remote_copy(
             src_ref=halo_out,
-            dst_ref=halo_buf.at[y],
+            dst_ref=halo_in,
             send_sem=send_edge.at[1],
             recv_sem=recv_edge.at[1],
             device_id=(sub, tm - 1),
             device_id_type=MESH,
         )
 
-    def halo_copy(d, source):
-        return pltpu.make_async_remote_copy(
-            src_ref=halo_buf.at[y],
-            dst_ref=halo_buf.at[source],
-            send_sem=send_halo.at[d],
-            recv_sem=recv_halo.at[source],
-            device_id=(along_y(d), tm),
-            device_id_type=MESH,
-        )
-
     @pl.when(tm > 0)
     def _():
         hop_copy().start()
+
+    for d in FAR_FIRST:
+        lag_copy(d, z).start()
+
+    @pl.when(last)
+    def _():
+        own_buf[y, :, length:] = jnp.zeros((per, LANES), jnp.bfloat16)
+
+    @pl.when(jnp.logical_not(last))
+    def _():
+        hop_copy().wait_recv()
+        halo = halo_in[...].astype(jnp.float32)
+        edge = jnp.where(iota((per, LANES), 1) >= EDGE, halo, 0.0)
+        tail = own_buf[y, :, length - LANES : length].astype(jnp.float32) + edge
+        own_buf[y, :, length - LANES : length] = tail.astype(jnp.bfloat16)
+        own_buf[y, :, length:] = halo_in[...]
 
     for d in FAR_FIRST:
         own_copy(d, y).start()
-        lag_copy(d, z).start()
-
-    @pl.when(last)
-    def _():
-        halo_buf[...] = jnp.zeros(halo_buf.shape, halo_buf.dtype)
-
-    @pl.when(jnp.logical_not(last))
-    def _():
-        hop_copy().wait_recv()
-        for d in FAR_FIRST:
-            halo_copy(d, y).start()
 
     rows = RING * per
     for d in NEAR_FIRST:
@@ -176,7 +169,7 @@
 
     for d in NEAR_FIRST:
         own_copy(d, lax.rem(y + d, RING)).wait_recv()
-    turned[:length] = own_buf[...].reshape(rows, length).astype(jnp.float32).T
+    turned[...] = own_buf[...].reshape(rows, wide).astype(jnp.float32).T
 
     def part_copy(t, d, source):
         return pltpu.make_async_remote_copy(
@@ -198,39 +191,23 @@
             device_id_type=MESH,
         )
 
-    def add_halo():
-        @pl.when(jnp.logical_not(last))
-        def _():
-            for d in NEAR_FIRST:
-                halo_copy(d, lax.rem(y + d, RING)).wait_recv()
-
-        halo = halo_buf[...].reshape(rows, LANES).astype(jnp.float32)
-        edge = jnp.where(iota((rows, LANES), 1) >= EDGE, halo, 0.0)
-        tail = own_buf[:, :, length - LANES :].reshape(rows, LANES).astype(jnp.float32) + edge
-        turned[length - LANES : length] = tail.astype(jnp.bfloat16).astype(jnp.float32).T
-        turned[length:] = halo.T
-
     tiles = length // LANES
 
-    def tile(t, carry):
-        pl.when(t == tiles - 1)(add_halo)
-        masks, windows = [], []
-        for j in range(OMAX + 1):
-            masks.append(jnp.where(table == jnp.bfloat16(j), jnp.bfloat16(1), jnp.bfloat16(0)))
-            windows.append(turned[pl.ds(t * LANES + j, LANES), :].astype(jnp.bfloat16))
-        total = jnp.dot(
-            jnp.concatenate(windows, axis=1),
-            jnp.concatenate(masks, axis=0),
-            preferred_element_type=jnp.float32,
-        )
-        part_buf[t] = total.T.astype(jnp.bfloat16).reshape(RING, dms, LANES)
+    masks, windows = [], []
+    for j in range(OMAX + 1):
+        masks.append(jnp.where(table == jnp.bfloat16(j), jnp.bfloat16(1), jnp.bfloat16(0)))
+        windows.append(turned[j : j + length, :].astype(jnp.bfloat16))
+    total = jnp.dot(
+        jnp.concatenate(windows, axis=1),
+        jnp.concatenate(masks, axis=0),
+        preferred_element_type=jnp.float32,
+    )
+    for t in range(tiles):
+        tile = total[t * LANES : (t + 1) * LANES].T
+        part_buf[t] = tile.astype(jnp.bfloat16).reshape(RING, dms, LANES)
         for d in FAR_FIRST:
             part_copy(t, d, z).start()
-
         sum_buf[t, z] = part_buf[t, z]
-        return carry
-
-    lax.fori_loop(0, tiles, tile, 0)
 
     def finish(t):
         for d in NEAR_FIRST:
@@ -266,11 +243,6 @@
         lag_copy(d, z).wait_send()
         for t in range(tiles):
             part_copy(t, d, z).wait_send()
-
-    @pl.when(jnp.logical_not(last))
-    def _():
-        for d in NEAR_FIRST:
-            halo_copy(d, y).wait_send()
 
     @pl.when(tm > 0)
     def _():
@@ -321,16 +293,16 @@
                 pltpu.VMEM((dms, nsub), jnp.int32),
                 pltpu.VMEM((RING, dms, LANES), bf16),
                 pltpu.VMEM((RING, dms, LANES), bf16),
-                pltpu.VMEM((RING, per, length), bf16),
+                pltpu.VMEM((RING, per, length + LANES), bf16),
                 pltpu.VMEM((per, LANES), bf16),
-                pltpu.VMEM((RING, per, LANES), bf16),
+                pltpu.VMEM((per, LANES), bf16),
                 pltpu.VMEM((length + LANES, RING * per), jnp.float32),
                 pltpu.VMEM((length // LANES, RING, dms, LANES), bf16),
                 pltpu.VMEM((length // LANES, RING, dms, LANES), bf16),
                 pltpu.VMEM((dms, LANES), bf16),
                 pltpu.VMEM((dms, LANES), bf16),
             ]
-            + [dma] * 6
+            + [dma] * 4
             + [pltpu.SemaphoreType.DMA((RING * (length // LANES),))] * 2
             + [pltpu.SemaphoreType.DMA((2,))] * 2
             + [pltpu.SemaphoreType.DMA((3,))],

time: 30.8 us -> 31.8 us (1.032)
  Pallas kernels: 30.6 us -> 31.6 us
    pallas_call x1, Pallas kernels: 28.9 us -> 29.9 us  [per_device(): pl.pallas_call(functools.partial(dedisperse_kernel, scale, blocks), out_s...]
where the time goes in v8:
time: 31.8 us; the launch traced here: 31.6 us
  Pallas kernels  31.6 us (99%)
    pallas_call x1, Pallas kernels, per_device(): pl.pallas_call(functools.partial(dedisperse_kernel, scale, blocks), out_s...  29.9 us
    pallas_call x1, Pallas kernels, per_device(): pl.pallas_call(boxcar_kernel, out_shape=jax.ShapeDtypeStruct((dms * count...  1.71 us

profile of v8, /device:TPU:1, one launch (start us, length us, event | category | flops | bytes accessed | tf_op | source)
XLA Modules:
  0.0 31.6 jit_solution(1923854000267132898)
XLA Ops:
  0.0 29.9 %shard_map.46.series_ref = bf16[32,384]{1,0:T(8,128)(2,1)} custom-call(bf16[256,256]{1,0:T(8,128)(2,1)} %bitcast.5, s32[1,256]{1,0:T(1,128)} %bitcast.6, s32[32,1024]{1,0:T(8,128)} %offsets_hbm.1), custom_call_target="tpu_custom_call" | custom-call | tf_op jit(solution)/shard_map/pallas_call | solution.py:285
  29.9 1.7 %shard_map.47 = f32[256,256]{1,0:T(8,128)} custom-call(s32[8]{0:T(128)} %widths_ref.1, bf16[32,384]{1,0:T(8,128)(2,1)} %shard_map.46.series_ref), custom_call_target="tpu_custom_call" | custom-call | tf_op jit(solution)/shard_map/pallas_call | solution.py:312

commit v9 on v5

--- a/solution.py
+++ b/solution.py
@@ -54,6 +54,7 @@
     send_edge,
     recv_edge,
     load,
+    ready,
 ):
     sub = lax.axis_index("sub")
     tm = lax.axis_index("tm")
@@ -84,8 +85,11 @@
 
     @pl.when(jnp.logical_not(last))
     def _():
-        for d in FAR_FIRST + (0,):
-            pl.semaphore_signal(barrier, inc=1, device_id=(along_y(d), tm + 1), device_id_type=MESH)
+        pl.semaphore_signal(barrier, inc=1, device_id=(sub, tm + 1), device_id_type=MESH)
+
+    @pl.when(tm > 0)
+    def _():
+        pl.semaphore_signal(barrier, inc=1, device_id=(sub, tm - 1), device_id_type=MESH)
 
     fetch(2, offsets_hbm, offsets_ref).wait()
     for g in range(RING):
@@ -109,10 +113,11 @@
         iota((per, LANES), 1) < EDGE, summed[:, LANES : 2 * LANES], summed[:, :LANES]
     ).astype(jnp.bfloat16)
 
-    pl.semaphore_wait(
-        barrier,
-        2 * (RING - 1) + jnp.where(first, 0, RING),
-    )
+    pl.semaphore_wait(barrier, 2 * (RING - 1) + jnp.where(first, 0, 1) + jnp.where(last, 0, 1))
+
+    @pl.when(jnp.logical_not(last))
+    def _():
+        pl.semaphore_signal(ready, inc=1, device_id=(sub, tm + 1), device_id_type=MESH)
 
     def lag_copy(d, source):
         g = lax.rem(z + d, RING)
@@ -151,6 +156,7 @@
 
     @pl.when(tm > 0)
     def _():
+        pl.semaphore_wait(ready, 1)
         for d in FAR_FIRST + (0,):
             halo_copy(d, y).start()
 
@@ -158,14 +164,14 @@
     def _():
         halo_buf[...] = jnp.zeros(halo_buf.shape, halo_buf.dtype)
 
+    rows = RING * per
     for d in NEAR_FIRST:
         lag_copy(d, lax.rem(z + d, RING)).wait_recv()
+    table = lags[...].reshape(RING * dms, rows).astype(jnp.float32).T.astype(jnp.bfloat16)
+
+    for d in NEAR_FIRST:
         own_copy(d, lax.rem(y + d, RING)).wait_recv()
-
-    rows = RING * per
     turned[:length] = own_buf[...].reshape(rows, length).astype(jnp.float32).T
-
-    table = lags[...].reshape(RING * dms, rows).astype(jnp.float32).T.astype(jnp.bfloat16)
 
     def part_copy(t, d, source):
         return pltpu.make_async_remote_copy(
@@ -318,7 +324,7 @@
             + [dma] * 6
             + [pltpu.SemaphoreType.DMA((RING * (length // LANES),))] * 2
             + [pltpu.SemaphoreType.DMA((1,))] * 2
-            + [pltpu.SemaphoreType.DMA((3,))],
+            + [pltpu.SemaphoreType.DMA((3,)), pltpu.SemaphoreType.REGULAR],
             compiler_params=pltpu.CompilerParams(collective_id=0, has_side_effects=True),
         )(data[0], delays[None, :], offsets)
         count = widths.shape[0]

time: 31.2 us -> 31.2 us (level)
  no operation moved by 1% of the time
where the time goes in v9:
time: 31.2 us; the launch traced here: 31 us
  Pallas kernels  31 us (99%)
    pallas_call x1, Pallas kernels, per_device(): pl.pallas_call(functools.partial(dedisperse_kernel, scale, blocks), out_s...  29.3 us
    pallas_call x1, Pallas kernels, per_device(): pl.pallas_call(boxcar_kernel, out_shape=jax.ShapeDtypeStruct((dms * count...  1.71 us

profile of v9, /device:TPU:1, one launch (start us, length us, event | category | flops | bytes accessed | tf_op | source)
XLA Modules:
  0.0 31.0 jit_solution(4072242921270983841)
XLA Ops:
  0.0 29.3 %shard_map.46.series_ref = bf16[32,384]{1,0:T(8,128)(2,1)} custom-call(bf16[256,256]{1,0:T(8,128)(2,1)} %bitcast.5, s32[1,256]{1,0:T(1,128)} %bitcast.6, s32[32,1024]{1,0:T(8,128)} %offsets_hbm.1), custom_call_target="tpu_custom_call" | custom-call | tf_op jit(solution)/shard_map/pallas_call | solution.py:304
  29.3 1.7 %shard_map.47 = f32[256,256]{1,0:T(8,128)} custom-call(s32[8]{0:T(128)} %widths_ref.1, bf16[32,384]{1,0:T(8,128)(2,1)} %shard_map.46.series_ref), custom_call_target="tpu_custom_call" | custom-call | tf_op jit(solution)/shard_map/pallas_call | solution.py:331

commit v10 on v6

--- a/solution.py
+++ b/solution.py
@@ -334,7 +334,7 @@
             + [pltpu.SemaphoreType.DMA((RING * (length // LANES),))] * 2
             + [pltpu.SemaphoreType.DMA((2,))] * 2
             + [pltpu.SemaphoreType.DMA((3,))],
-            compiler_params=pltpu.CompilerParams(collective_id=0, has_side_effects=True),
+            compiler_params=pltpu.CompilerParams(collective_id=0, has_side_effects=True, vmem_limit_bytes=16 * 2**20),
         )(data[0], delays[None, :], offsets)
         count = widths.shape[0]
         out = pl.pallas_call(
@@ -342,6 +342,7 @@
             out_shape=jax.ShapeDtypeStruct((dms * count, length), jnp.float32),
             in_specs=[pl.BlockSpec(memory_space=pltpu.SMEM), vmem],
             out_specs=vmem,
+            compiler_params=pltpu.CompilerParams(vmem_limit_bytes=16 * 2**20),
             scratch_shapes=[pltpu.VMEM((length // LANES, dms * count, LANES), jnp.float32)],
         )(widths, series)
         return out.reshape(dms, 1, count, length)

time: 30.8 us -> 33 us (1.071)
  local copies, waits for them, and re-layouts: 0 us -> 2.49 us
    unnamed x0 -> x8, local copies, waits for them, and re-layouts: none -> 2.49 us
where the time goes in v10:
time: 33 us; the launch traced here: 32.8 us
  Pallas kernels  30.3 us (92%)
  local copies, waits for them, and re-layouts  2.49 us (8%)
    pallas_call x1, Pallas kernels, per_device(): pl.pallas_call(functools.partial(dedisperse_kernel, scale, blocks), out_s...  28.8 us
    unnamed x8, local copies, waits for them, and re-layouts  2.49 us
    pallas_call x1, Pallas kernels, per_device(): pl.pallas_call(boxcar_kernel, out_shape=jax.ShapeDtypeStruct((dms * count...  1.5 us

profile of v10, /device:TPU:1, one launch (start us, length us, event | category | flops | bytes accessed | tf_op | source)
XLA Modules:
  0.0 32.8 jit_solution(7781832134940967605)
XLA Ops:
  0.0 0.0 copy-start.2
  0.0 0.7 %copy-done.2 = s32[256]{0:T(256)S(1)} copy-done((s32[256]{0:T(256)S(1)}, s32[256]{0:T(256)}, u32[]{:S(2)}) %copy-start.2) | copy-done | bytes 1048
  0.7 0.0 copy-start
  0.7 0.9 %copy-done = bf16[1,256,256]{2,1,0:T(8,128)(2,1)S(1)} copy-done((bf16[1,256,256]{2,1,0:T(8,128)(2,1)S(1)}, bf16[1,256,256]{2,1,0:T(8,128)(2,1)}, u32[]{:S(2)}) %copy-start) | copy-done | bytes 131096
  1.6 0.0 copy-start.1
  1.6 0.9 %copy-done.1 = s32[32,1024]{1,0:T(8,128)S(1)} copy-done((s32[32,1024]{1,0:T(8,128)S(1)}, s32[32,1024]{1,0:T(8,128)}, u32[]{:S(2)}) %copy-start.1) | copy-done | bytes 131096
  2.5 0.0 copy-start.3
  2.5 28.8 %shard_map.46.series_ref = bf16[32,384]{1,0:T(8,128)(2,1)S(1)} custom-call(bf16[256,256]{1,0:T(8,128)(2,1)S(1)} %bitcast.5, s32[1,256]{1,0:T(1,128)S(1)} %bitcast.6, s32[32,1024]{1,0:T(8,128)S(1)} %copy-done.1), custom_call_target="tpu_custom_call" | custom-call | tf_op jit(solution)/shard_map/pallas_call | solution.py:313
  31.3 0.0 copy-done.3
  31.3 1.5 %shard_map.47 = f32[256,256]{1,0:T(8,128)} custom-call(s32[8]{0:T(128)S(1)} %copy-done.3, bf16[32,384]{1,0:T(8,128)(2,1)S(1)} %shard_map.46.series_ref), custom_call_target="tpu_custom_call" | custom-call | tf_op jit(solution)/shard_map/pallas_call | solution.py:340
Async XLA Ops:
  0.0 0.7 %copy-start.2 = (s32[256]{0:T(256)S(1)}, s32[256]{0:T(256)}, u32[]{:S(2)}) copy-start(s32[256]{0:T(256)} %param.5) | copy-start | bytes 3076
  0.7 0.9 %copy-start = (bf16[1,256,256]{2,1,0:T(8,128)(2,1)S(1)}, bf16[1,256,256]{2,1,0:T(8,128)(2,1)}, u32[]{:S(2)}) copy-start(bf16[1,256,256]{2,1,0:T(8,128)(2,1)} %param.4) | copy-start | bytes 393220
  1.6 0.9 %copy-start.1 = (s32[32,1024]{1,0:T(8,128)S(1)}, s32[32,1024]{1,0:T(8,128)}, u32[]{:S(2)}) copy-start(s32[32,1024]{1,0:T(8,128)} %offsets_hbm.1) | copy-start | bytes 393220
  2.5 28.8 %copy-start.3 = (s32[8]{0:T(128)S(1)}, s32[8]{0:T(128)}, u32[]{:S(2)}) copy-start(s32[8]{0:T(128)} %widths_ref.1) | copy-start | bytes 100
